TPU v7x, 512 devices: a whole 4x4x16 slice. The times are simulated.
512 devices in a mesh: grp: 8 (over x, core), path: 64 (over z, y).
Axes of the slice: x: 4, y: 4, z: 16, core: 2. Of those that a mesh axis runs over, the one named last changes fastest.
Arguments:
- normals: float32 [32, 8388608], P(None, ('grp', 'path')), may hold values from -10.1 to 10.1
- spot_today: float32 [32], replicated, may hold values from 0.5 to 2
- volatility: float32 [32], replicated, may hold values from 0.1 to 0.5
- weights: float32 [32], replicated, may hold values from 0.5 to 1.5
- cash_flows: float32 [8388608], P(('grp', 'path')), may hold values from -300 to 300
- exercise: int32 [8388608], P(('grp', 'path')), may hold values 0 or 1
Outputs:
- path_value: float32 [8388608], P(('grp', 'path'))
- state_cot: float32 [32, 8388608], P(None, ('grp', 'path'))
- flow_cot: float32 [8388608], P(('grp', 'path'))
- greeks: float32 [2, 32], replicated
All inputs are finite; a program needn't handle non-finite values. No bound on the sum of `exercise` on one device may be relied on, other than what follows from the above.
Results may differ from a plain program's by a relative error of at most 0.0003.
Values sent between devices are 32-bit elements; how exact they have to be, the bound alone decides.
A program may use at most 64 MiB of HBM per device.

v0:
```python
import math
import jax
import jax.numpy as jnp
from jax import lax
from jax.sharding import PartitionSpec as P

expiry_time = 0.5
root_time = math.sqrt(0.5)
inv_root_two = 1.0 / math.sqrt(2.0)
notional = 20.0
soft_width = 0.02


def path_state(normals, spot_today, volatility):
    return spot_today[:, None] * jnp.exp(
        volatility[:, None] * (root_time * normals) - 0.5 * expiry_time * volatility[:, None] ** 2
    )


def basis_rows(state, spot_today, volatility):
    scaled = (state / spot_today[:, None] - 1.0) / (volatility[:, None] * root_time)
    leading = jnp.ones_like(scaled[:1])
    squares = (scaled * scaled - 1.0) * inv_root_two
    neighbour = scaled * jnp.roll(scaled, -1, axis=0)
    bounded = jnp.tanh(scaled[:-1])
    return jnp.concatenate([leading, scaled, squares, neighbour, bounded], axis=0)


def payoff(state, spot_today, weights):
    basket = jnp.sum(weights[:, None] * state, axis=0) / jnp.sum(weights * spot_today)
    return notional * soft_width * jax.nn.softplus((basket - 1.0) / soft_width)


def chol_solve(factor, rhs):
    first = lax.linalg.triangular_solve(factor, rhs, left_side=True, lower=True)
    return lax.linalg.triangular_solve(factor, first, left_side=True, lower=True, transpose_a=True)


def per_device(normals, spot_today, volatility, weights, cash_flows, exercise):
    assets, local_paths = normals.shape
    features = 4 * assets
    block_width = math.gcd(local_paths, 1024)
    block_count = local_paths // block_width
    path_total = local_paths * lax.axis_size("grp") * lax.axis_size("path")
    highest = lax.Precision.HIGHEST
    contract_last = (((1,), (1,)), ((), ()))

    def block_inputs(block_index):
        block_start = block_index * block_width
        draw_block = lax.dynamic_slice_in_dim(normals, block_start, block_width, 1)
        flow_block = lax.dynamic_slice_in_dim(cash_flows, block_start, block_width, 0)
        taken_flag = lax.dynamic_slice_in_dim(exercise, block_start, block_width, 0).astype(
            jnp.float32
        )
        return (draw_block, flow_block, taken_flag)

    def gram_step(block_index, running):
        gram_acc, moment_acc = running
        draw_block, flow_block, taken_flag = block_inputs(block_index)
        basis_block = basis_rows(
            path_state(draw_block, spot_today, volatility), spot_today, volatility
        )
        gram_acc = gram_acc + lax.dot_general(
            basis_block,
            basis_block,
            contract_last,
            precision=highest,
            preferred_element_type=jnp.float32,
        )
        targets = jnp.stack([flow_block, 1.0 - taken_flag])
        moment_acc = moment_acc + lax.dot_general(
            targets,
            basis_block,
            contract_last,
            precision=highest,
            preferred_element_type=jnp.float32,
        )
        return (gram_acc, moment_acc)

    zero_gram = jnp.zeros((features, features), jnp.float32)
    zero_moment = jnp.zeros((2, features), jnp.float32)
    gram_acc, moment_acc = lax.fori_loop(0, block_count, gram_step, (zero_gram, zero_moment))
    gram_sum, moment_sum = lax.psum((gram_acc, moment_acc), ("grp", "path"))
    gram_mean = gram_sum / path_total
    moment_mean = moment_sum / path_total
    factor = jnp.linalg.cholesky(gram_mean)
    coefficients = chol_solve(factor, moment_mean.T)
    regression = coefficients[:, 0]
    multiplier = coefficients[:, 1]
    coef_rows = coefficients.T

    def adjoint_step(block_index, running):
        value_out, state_out, flow_out, greek_acc = running
        draw_block, flow_block, taken_flag = block_inputs(block_index)
        state, path_back = jax.vjp(
            lambda spot_level, spread: path_state(draw_block, spot_level, spread),
            spot_today,
            volatility,
        )
        (basis_block, reward), feature_back = jax.vjp(
            lambda current, spot_level, spread: (
                basis_rows(current, spot_level, spread),
                payoff(current, spot_level, weights),
            ),
            state,
            spot_today,
            volatility,
        )
        fitted = lax.dot_general(
            coef_rows,
            basis_block,
            (((1,), (0,)), ((), ())),
            precision=highest,
            preferred_element_type=jnp.float32,
        )
        continuation = fitted[0]
        lam_phi = fitted[1]
        value_block = taken_flag * reward + (1.0 - taken_flag) * continuation
        rows_bar = (
            multiplier[:, None] * (flow_block - continuation)[None, :]
            + regression[:, None] * (1.0 - taken_flag - lam_phi)[None, :]
        )
        state_bar, spot_bar, spread_bar = feature_back((rows_bar, taken_flag))
        spot_path, spread_path = path_back(state_bar)
        greek_acc = greek_acc + jnp.stack([spot_bar + spot_path, spread_bar + spread_path])
        block_start = block_index * block_width
        value_out = lax.dynamic_update_slice_in_dim(value_out, value_block, block_start, 0)
        state_out = lax.dynamic_update_slice_in_dim(state_out, state_bar, block_start, 1)
        flow_out = lax.dynamic_update_slice_in_dim(flow_out, lam_phi, block_start, 0)
        return (value_out, state_out, flow_out, greek_acc)

    start_outs = (
        jnp.zeros((local_paths,), jnp.float32),
        jnp.zeros((assets, local_paths), jnp.float32),
        jnp.zeros((local_paths,), jnp.float32),
        jnp.zeros((2, assets), jnp.float32),
    )
    path_value, state_cot, flow_cot, greek_acc = lax.fori_loop(
        0, block_count, adjoint_step, start_outs
    )
    greeks = lax.psum(greek_acc, ("grp", "path")) / path_total
    return (path_value, state_cot, flow_cot, greeks)


def solution(mesh):
    in_specs = (P(None, ("grp", "path")), P(), P(), P(), P(("grp", "path")), P(("grp", "path")))
    out_specs = (P(("grp", "path")), P(None, ("grp", "path")), P(("grp", "path")), P())
    return jax.shard_map(
        per_device, mesh=mesh, in_specs=in_specs, out_specs=out_specs, check_vma=False
    )
```

profile of v0, /device:TPU:1, one launch (start us, length us, event | category | flops | bytes accessed | tf_op | source)
XLA Modules:
  0.0 799.2 jit_solution(2905008628798093460)
XLA Ops:
  7.9 80.4 %while.42 = (s32[]{:T(128)}, f32[128,128]{1,0:T(8,128)S(1)}, f32[2,128]{1,0:T(2,128)S(1)}, f32[32]{0:T(128)}, f32[32,16384]{1,0:T(8,128)}, /*index=5*/f32[32]{0:...) while((s32[]{:T(128)}, f32[128,128]{1,0:T(8,128)S(1)}, ...), condition=%wide.region_1.2_spmd.clone, body=%wide.region_0.1_spmd.clone.sunk | while | flops 204870208 | bytes 3562582 | solution.py:82
  9.9 1.0 add_multiply_fusion.5
  20.0 1.0 add_multiply_fusion.5
  45.1 1.0 add_multiply_fusion.5
  55.2 1.0 add_multiply_fusion.5
  60.2 1.0 add_multiply_fusion.5
  65.2 1.0 add_multiply_fusion.5
  70.3 1.0 add_multiply_fusion.5
  80.3 1.0 add_multiply_fusion.5
  89.1 1.3 multiply_bitcast_fusion.2
  91.7 111.2 %psum.22 = f32[2,128]{1,0:T(2,128)S(1)} all-reduce(f32[2,128]{1,0:T(2,128)S(1)} %get-tuple-element.642), channel_id=1, replica_groups=mesh['grp'=8,'path'=64] {'grp','path'}, use_global_device_ids=true, to_apply=%region_5.6 | all-reduce | flops 256 | bytes 2048 | tf_op jit(solution)/shard_map/psum | solution.py:83
  202.9 340.4 %all-reduce.5.cloned.1.call-done = f32[128,128]{0,1:T(8,128)} async-done(((f32[128,128]{0,1:T(8,128)}), f32[128,128]{0,1:T(8,128)}) %all-reduce.5.cloned.1.call-update) | async-done | bytes 65552 | tf_op jit(solution)/shard_map/psum | solution.py:83
  545.1 11.7 %cholesky.15 = f32[128,128]{1,0:T(8,128)S(1)} custom-call(f32[128,128]{1,0:T(8,128)S(1)} %fusion.19), custom_call_target="Cholesky" | custom-call | tf_op jit(solution)/shard_map/jit(cholesky)/cholesky | solution.py:86
  558.1 9.8 %custom-call.8 = f32[1,128,128]{1,2,0:T(8,128)S(1)} custom-call(f32[1,128,128]{2,1,0:T(8,128)S(1)} %fusion.14), custom_call_target="InvertDiagBlocksLowerTriangular" | custom-call | tf_op jit(solution)/shard_map/triangular_solve | solution.py:36
  568.7 121.5 %while.43 = (s32[]{:T(128)}, f32[16384]{0:T(1024)S(1)}, f32[32,16384]{1,0:T(8,128)S(1)}, f32[16384]{0:T(1024)S(1)}, f32[2,32]{1,0:T(2,128)S(1)}, /*index=5*/s32[...) while((s32[]{:T(128)}, f32[16384]{0:T(1024)S(1)}, ...), condition=%wide.region_15.16_spmd.clone, body=%wide.region_7.15_spmd.clone.sunk | while | flops 5333607 | bytes 5730625 | solution.py:138
  568.8 1.0 add_multiply_fusion.6
  571.3 2.0 multiply_reduce_fusion.8
  574.8 1.3 fusion.49
  576.4 1.0 add_multiply_fusion.6
  578.9 2.0 multiply_reduce_fusion.8
  582.4 1.3 fusion.49
  584.0 1.0 add_multiply_fusion.6
  586.5 2.0 multiply_reduce_fusion.8
  590.0 1.3 fusion.49
  591.6 1.0 add_multiply_fusion.6
  594.1 2.0 multiply_reduce_fusion.8
  597.6 1.3 fusion.49
  599.2 1.0 add_multiply_fusion.6
  601.7 2.0 multiply_reduce_fusion.8
  605.2 1.3 fusion.49
  606.7 1.0 add_multiply_fusion.6
  609.3 2.0 multiply_reduce_fusion.8
  612.8 1.3 fusion.49
  614.3 1.0 add_multiply_fusion.6
  616.9 2.0 multiply_reduce_fusion.8
  620.4 1.3 fusion.49
  621.9 1.0 add_multiply_fusion.6
  624.5 2.0 multiply_reduce_fusion.8
  628.0 1.3 fusion.49
  629.5 1.0 add_multiply_fusion.6
  632.1 2.0 multiply_reduce_fusion.8
  635.6 1.3 fusion.49
  637.1 1.0 add_multiply_fusion.6
  639.7 2.0 multiply_reduce_fusion.8
  643.2 1.3 fusion.49
  644.7 1.0 add_multiply_fusion.6
  647.3 2.0 multiply_reduce_fusion.8
  650.8 1.3 fusion.49
  652.3 1.0 add_multiply_fusion.6
  654.9 2.0 multiply_reduce_fusion.8
  658.4 1.3 fusion.49
  659.9 1.0 add_multiply_fusion.6
  662.5 2.0 multiply_reduce_fusion.8
  666.0 1.3 fusion.49
  667.5 1.0 add_multiply_fusion.6
  670.1 2.0 multiply_reduce_fusion.8
  673.6 1.3 fusion.49
  675.1 1.0 add_multiply_fusion.6
  677.7 2.0 multiply_reduce_fusion.8
  681.2 1.3 fusion.49
  682.7 1.0 add_multiply_fusion.6
  685.2 2.0 multiply_reduce_fusion.8
  688.8 1.3 fusion.49
  690.3 101.5 %psum.23 = f32[2,32]{1,0:T(2,128)S(1)} all-reduce(f32[2,32]{1,0:T(2,128)S(1)} %get-tuple-element.646), channel_id=1, replica_groups=mesh['grp'=8,'path'=64] {'grp','path'}, use_global_device_ids=true, to_apply=%region_16.17 | all-reduce | flops 64 | bytes 512 | tf_op jit(solution)/shard_map/psum | solution.py:141
  (520 shorter events, 115.2 us)
Async XLA Ops:
  7.2 536.1 %all-reduce.5.cloned.1.call-start = ((), (), s32[]{:S(2)}) async-start(), calls=%async_computation | async-start | bytes 131072 | tf_op jit(solution)/shard_map/psum | solution.py:83
  7.9 81.2 %copy-start.1 = (f32[32]{0:T(128)S(1)}, f32[32]{0:T(128)}, u32[]{:S(2)}) copy-start(f32[32]{0:T(128)} %param.13) | copy-start | bytes 388
  88.3 480.4 %copy-start.2 = (f32[32]{0:T(128)S(1)}, f32[32]{0:T(128)}, u32[]{:S(2)}) copy-start(f32[32]{0:T(128)} %get-tuple-element.1153) | copy-start | bytes 388
  88.3 480.4 %copy-start.5 = (f32[32]{0:T(128)S(1)}, f32[32]{0:T(128)}, u32[]{:S(2)}) copy-start(f32[32]{0:T(128)} %get-tuple-element.1154) | copy-start | bytes 388
  690.2 102.1 %copy-start = (f32[32,16384]{1,0:T(8,128)}, f32[32,16384]{1,0:T(8,128)S(1)}, u32[]{:S(2)}) copy-start(f32[32,16384]{1,0:T(8,128)S(1)} %get-tuple-element.638) | copy-start | bytes 6291460
  690.3 102.1 %copy-start.3 = (f32[16384]{0:T(1024)}, f32[16384]{0:T(1024)S(1)}, u32[]{:S(2)}) copy-start(f32[16384]{0:T(1024)S(1)} %get-tuple-element.639) | copy-start | bytes 196612
  690.3 102.1 %copy-start.4 = (f32[16384]{0:T(1024)}, f32[16384]{0:T(1024)S(1)}, u32[]{:S(2)}) copy-start(f32[16384]{0:T(1024)S(1)} %get-tuple-element.637) | copy-start | bytes 196612
Sparse Core Ops, SparseCore 0:
  89.2 454.0 all-reduce.4
where the time goes:
time: 803 us; the launch traced here: 799 us
  waiting for transfers between devices  340 us (42%)
  blocking collectives  213 us (27%)
  other arithmetic  151 us (19%)
  local copies, waits for them, and re-layouts  40.1 us (5%)
  matrix products  24.6 us (3%)
  between operations  15.5 us (2%)
  loops' own time  14.4 us (2%)
    psum x1, waiting for transfers between devices, per_device(): gram_sum, moment_sum = lax.psum((gram_acc, moment_acc), ('grp', 'path'))  340 us
    psum x1, blocking collectives, per_device(): gram_sum, moment_sum = lax.psum((gram_acc, moment_acc), ('grp', 'path'))  111 us
    psum x1, blocking collectives, per_device(): greeks = lax.psum(greek_acc, ('grp', 'path')) / path_total  101 us
    mul x32, other arithmetic, basis_rows(): squares = (scaled * scaled - 1.0) * inv_root_two  33.1 us
    reduce_sum x16, other arithmetic, payoff(): jnp.sum(weights[:, None] * state, axis=0) / jnp.sum(weights * spot_today)  31.9 us
    concatenate x32, local copies, waits for them, and re-layouts, basis_rows(): jnp.concatenate([leading, scaled, squares, neighbour, bounded], axis=0)  21.9 us
    reduce_sum x16, other arithmetic, path_state(): volatility[:, None] * (root_time * normals)  21.4 us
  transfers between devices with their start and end apart: 1, of which 1 were waited for; matrix products, arithmetic and copies ran while one was open for 0% of the time, Pallas kernels for 0%

commit v1 on v0

--- a/solution.py
+++ b/solution.py
@@ -80,7 +80,7 @@
     zero_gram = jnp.zeros((features, features), jnp.float32)
     zero_moment = jnp.zeros((2, features), jnp.float32)
     gram_acc, moment_acc = lax.fori_loop(0, block_count, gram_step, (zero_gram, zero_moment))
-    gram_sum, moment_sum = lax.psum((gram_acc, moment_acc), ("grp", "path"))
+    gram_sum, moment_sum = lax.psum(lax.psum((gram_acc, moment_acc), "path"), "grp")
     gram_mean = gram_sum / path_total
     moment_mean = moment_sum / path_total
     factor = jnp.linalg.cholesky(gram_mean)

time: 803 us -> 769 us (0.958)
  waiting for transfers between devices: 340 us -> 257 us
  blocking collectives: 213 us -> 263 us
    psum x1 -> x2, waiting for transfers between devices: 340 us -> 257 us  [the longest x1 257 us: per_device(): lax.psum((gram_acc, moment_acc), 'path')]
    psum x1 -> x2, blocking collectives: 111 us -> 165 us  [the longest x1 113 us: per_device(): lax.psum((gram_acc, moment_acc), 'path')]
  transfers between devices with their start and end apart: 1 -> 2, of which waited for: 1 -> 1; matrix products, arithmetic and copies ran while one was open for 0% -> 0% of each run, Pallas kernels for 0% -> 0%
where the time goes in v1:
time: 769 us; the launch traced here: 766 us
  blocking collectives  263 us (34%)
  waiting for transfers between devices  257 us (33%)
  other arithmetic  151 us (20%)
  local copies, waits for them, and re-layouts  40.1 us (5%)
  matrix products  24.6 us (3%)
  between operations  15.5 us (2%)
  loops' own time  14.4 us (2%)
    psum x1, waiting for transfers between devices, per_device(): lax.psum((gram_acc, moment_acc), 'path')  257 us
    psum x1, blocking collectives, per_device(): lax.psum((gram_acc, moment_acc), 'path')  113 us
    psum x1, blocking collectives, per_device(): greeks = lax.psum(greek_acc, ('grp', 'path')) / path_total  98.7 us
    psum x1, blocking collectives, per_device(): lax.psum(lax.psum((gram_acc, moment_acc), 'path'), 'grp')  51.3 us
    mul x32, other arithmetic, basis_rows(): squares = (scaled * scaled - 1.0) * inv_root_two  33.1 us
    reduce_sum x16, other arithmetic, payoff(): jnp.sum(weights[:, None] * state, axis=0) / jnp.sum(weights * spot_today)  31.9 us
    concatenate x32, local copies, waits for them, and re-layouts, basis_rows(): jnp.concatenate([leading, scaled, squares, neighbour, bounded], axis=0)  21.9 us
    reduce_sum x16, other arithmetic, path_state(): volatility[:, None] * (root_time * normals)  21.4 us
  transfers between devices with their start and end apart: 2, of which 1 were waited for; matrix products, arithmetic and copies ran while one was open for 0% of the time, Pallas kernels for 0%

profile of v1, /device:TPU:1, one launch (start us, length us, event | category | flops | bytes accessed | tf_op | source)
XLA Modules:
  0.0 766.0 jit_solution(15858422025448748077)
XLA Ops:
  7.9 80.4 %while.42 = (s32[]{:T(128)}, f32[128,128]{1,0:T(8,128)S(1)}, f32[2,128]{1,0:T(2,128)S(1)}, f32[32]{0:T(128)}, f32[32,16384]{1,0:T(8,128)}, /*index=5*/f32[32]{0:...) while((s32[]{:T(128)}, f32[128,128]{1,0:T(8,128)S(1)}, ...), condition=%wide.region_1.2_spmd.clone, body=%wide.region_0.1_spmd.clone.sunk | while | flops 204870208 | bytes 3562582 | solution.py:82
  9.9 1.0 add_multiply_fusion.5
  20.0 1.0 add_multiply_fusion.5
  45.1 1.0 add_multiply_fusion.5
  55.2 1.0 add_multiply_fusion.5
  60.2 1.0 add_multiply_fusion.5
  65.2 1.0 add_multiply_fusion.5
  70.3 1.0 add_multiply_fusion.5
  89.1 256.7 %all-reduce.6.cloned.1.call-done = f32[128,128]{0,1:T(8,128)} async-done(((f32[128,128]{0,1:T(8,128)}), f32[128,128]{0,1:T(8,128)}) %all-reduce.6.cloned.1.call-update) | async-done | bytes 65552 | tf_op jit(solution)/shard_map/psum | solution.py:83
  345.9 1.3 multiply_bitcast_fusion.2
  348.5 113.2 %psum.37 = f32[2,128]{1,0:T(2,128)S(1)} all-reduce(f32[2,128]{1,0:T(2,128)S(1)} %get-tuple-element.642), channel_id=1, replica_groups=mesh['grp'=8,'path'=64] {'path'}, use_global_device_ids=true, to_apply=%region_6.7 | all-reduce | flops 256 | bytes 2048 | tf_op jit(solution)/shard_map/psum | solution.py:83
  461.7 51.3 %psum.38 = f32[2,128]{1,0:T(2,128)S(1)} all-reduce(f32[2,128]{1,0:T(2,128)S(1)} %psum.37), channel_id=1, replica_groups=mesh['grp'=8,'path'=64] {'grp'}, use_global_device_ids=true, to_apply=%region_7.8 | all-reduce | flops 256 | bytes 2048 | tf_op jit(solution)/shard_map/psum | solution.py:83
  514.8 11.7 %cholesky.15 = f32[128,128]{1,0:T(8,128)S(1)} custom-call(f32[128,128]{1,0:T(8,128)S(1)} %fusion.19), custom_call_target="Cholesky" | custom-call | tf_op jit(solution)/shard_map/jit(cholesky)/cholesky | solution.py:86
  527.8 9.8 %custom-call.8 = f32[1,128,128]{1,2,0:T(8,128)S(1)} custom-call(f32[1,128,128]{2,1,0:T(8,128)S(1)} %fusion.14), custom_call_target="InvertDiagBlocksLowerTriangular" | custom-call | tf_op jit(solution)/shard_map/triangular_solve | solution.py:36
  538.4 121.5 %while.43 = (s32[]{:T(128)}, f32[16384]{0:T(1024)S(1)}, f32[32,16384]{1,0:T(8,128)S(1)}, f32[16384]{0:T(1024)S(1)}, f32[2,32]{1,0:T(2,128)S(1)}, /*index=5*/s32[...) while((s32[]{:T(128)}, f32[16384]{0:T(1024)S(1)}, ...), condition=%wide.region_17.18_spmd.clone, body=%wide.region_9.17_spmd.clone.sunk | while | flops 5333607 | bytes 5730625 | solution.py:138
  538.4 1.0 add_multiply_fusion.6
  541.0 2.0 multiply_reduce_fusion.8
  544.5 1.3 fusion.49
  546.0 1.0 add_multiply_fusion.6
  548.6 2.0 multiply_reduce_fusion.8
  552.1 1.3 fusion.49
  553.6 1.0 add_multiply_fusion.6
  556.2 2.0 multiply_reduce_fusion.8
  559.7 1.3 fusion.49
  561.2 1.0 add_multiply_fusion.6
  563.8 2.0 multiply_reduce_fusion.8
  567.3 1.3 fusion.49
  568.8 1.0 add_multiply_fusion.6
  571.4 2.0 multiply_reduce_fusion.8
  574.9 1.3 fusion.49
  576.4 1.0 add_multiply_fusion.6
  579.0 2.0 multiply_reduce_fusion.8
  582.5 1.3 fusion.49
  584.0 1.0 add_multiply_fusion.6
  586.6 2.0 multiply_reduce_fusion.8
  590.1 1.3 fusion.49
  591.6 1.0 add_multiply_fusion.6
  594.2 2.0 multiply_reduce_fusion.8
  597.7 1.3 fusion.49
  599.2 1.0 add_multiply_fusion.6
  601.8 2.0 multiply_reduce_fusion.8
  605.3 1.3 fusion.49
  606.8 1.0 add_multiply_fusion.6
  609.4 2.0 multiply_reduce_fusion.8
  612.9 1.3 fusion.49
  614.4 1.0 add_multiply_fusion.6
  617.0 2.0 multiply_reduce_fusion.8
  620.5 1.3 fusion.49
  622.0 1.0 add_multiply_fusion.6
  624.6 2.0 multiply_reduce_fusion.8
  628.1 1.3 fusion.49
  629.6 1.0 add_multiply_fusion.6
  632.1 2.0 multiply_reduce_fusion.8
  635.7 1.3 fusion.49
  637.2 1.0 add_multiply_fusion.6
  639.7 2.0 multiply_reduce_fusion.8
  643.3 1.3 fusion.49
  644.8 1.0 add_multiply_fusion.6
  647.3 2.0 multiply_reduce_fusion.8
  650.9 1.3 fusion.49
  652.4 1.0 add_multiply_fusion.6
  654.9 2.0 multiply_reduce_fusion.8
  658.4 1.3 fusion.49
  660.0 98.7 %psum.39 = f32[2,32]{1,0:T(2,128)S(1)} all-reduce(f32[2,32]{1,0:T(2,128)S(1)} %get-tuple-element.646), channel_id=1, replica_groups=mesh['grp'=8,'path'=64] {'grp','path'}, use_global_device_ids=true, to_apply=%region_18.19 | all-reduce | flops 64 | bytes 512 | tf_op jit(solution)/shard_map/psum | solution.py:141
  (524 shorter events, 116.3 us)
Async XLA Ops:
  7.2 338.7 %all-reduce.6.cloned.1.call-start = ((), (), s32[]{:S(2)}) async-start(), calls=%async_computation | async-start | bytes 131072 | tf_op jit(solution)/shard_map/psum | solution.py:83
  7.9 338.0 %copy-start.1 = (f32[32]{0:T(128)S(1)}, f32[32]{0:T(128)}, u32[]{:S(2)}) copy-start(f32[32]{0:T(128)} %param.13) | copy-start | bytes 388
  88.3 450.1 %copy-start.2 = (f32[32]{0:T(128)S(1)}, f32[32]{0:T(128)}, u32[]{:S(2)}) copy-start(f32[32]{0:T(128)} %get-tuple-element.1154) | copy-start | bytes 388
  88.3 450.1 %copy-start.5 = (f32[32]{0:T(128)S(1)}, f32[32]{0:T(128)}, u32[]{:S(2)}) copy-start(f32[32]{0:T(128)} %get-tuple-element.1158) | copy-start | bytes 388
  89.1 423.9 %all-reduce.8.cloned.1.call-start = ((), (), s32[]{:S(2)}) async-start(), calls=%async_computation.1 | async-start | bytes 131072 | tf_op jit(solution)/shard_map/psum | solution.py:83
  659.9 99.3 %copy-start = (f32[32,16384]{1,0:T(8,128)}, f32[32,16384]{1,0:T(8,128)S(1)}, u32[]{:S(2)}) copy-start(f32[32,16384]{1,0:T(8,128)S(1)} %get-tuple-element.638) | copy-start | bytes 6291460
  659.9 99.2 %copy-start.3 = (f32[16384]{0:T(1024)}, f32[16384]{0:T(1024)S(1)}, u32[]{:S(2)}) copy-start(f32[16384]{0:T(1024)S(1)} %get-tuple-element.639) | copy-start | bytes 196612
  659.9 99.2 %copy-start.4 = (f32[16384]{0:T(1024)}, f32[16384]{0:T(1024)S(1)}, u32[]{:S(2)}) copy-start(f32[16384]{0:T(1024)S(1)} %get-tuple-element.637) | copy-start | bytes 196612
Sparse Core Ops, SparseCore 0:
  89.2 256.5 all-reduce.5
  348.1 78.6 all-reduce.7
